TPU v7x, 256 devices: a whole 4x4x8 slice. The times are simulated.
256 devices in a mesh: mp: 4 (over z_lo, core), fsdp: 16 (over y, x), dp: 4 (over z_hi).
Axes of the slice: x: 4, y: 4, z: 8 (z_hi: 4, z_lo: 2; z = z_hi * 2 + z_lo), core: 2. Of those that a mesh axis runs over, the one named last changes fastest.
Arguments:
- gen_noise: float32 [4, 4096, 128], P('dp', 'fsdp'), may hold values from -6 to 6
- renoise: float32 [4, 4096, 128], P('dp', 'fsdp'), may hold values from -120 to 120
- gen_step: int32 [4], P('dp'), may hold values from 250 to 999
- renoise_step: int32 [4], P('dp'), may hold values from 20 to 979
- text_pooled: bfloat16 [4, 768], P('dp'), may hold values from -6 to 6
- embed: bfloat16 [3, 64, 3072], replicated, may hold values from -0.75 to 0.75
- mod_weight: bfloat16 [3, 1024, 6144], P(None, None, 'fsdp'), may hold values from -0.1875 to 0.1875
- proj_weight: bfloat16 [3, 3072, 3072], P(None, 'fsdp', 'mp'), may hold values from -0.109375 to 0.109375
- unembed: bfloat16 [3, 64, 3072], P(None, None, 'mp'), may hold values from -0.109375 to 0.109375
Outputs:
- gen_grad: float32 [3072, 3072], P('fsdp', 'mp')
- score_gap: float32 [4, 4096, 128], P('dp', 'fsdp')
All inputs are finite; a program needn't handle non-finite values. Where the computation divides by a largest or mean magnitude, that divisor is 1e-20 or more.
Results may differ from a plain program's by a relative error of at most 0.03.
Values may be sent and summed in bfloat16 or wider, within the bound.
A program may use at most 128 MiB of HBM per device.

v0:
```python
import math
import jax
import jax.numpy as jnp
from jax import lax
from jax.sharding import PartitionSpec as P

D = 3072
CH = 64
TEMB = 256
GUIDANCE = 3.5
EPS_NORM = 1e-06
EPS_GAP = 1e-05


def sinusoid(timesteps):
    half_size = TEMB // 2
    frequency = jnp.exp(-math.log(10000.0) * jnp.arange(half_size, dtype=jnp.float32) / half_size)
    angles = timesteps.astype(jnp.float32)[:, None] * frequency[None, :]
    return jnp.concatenate([jnp.cos(angles), jnp.sin(angles)], axis=1)


def condition(timesteps, pooled):
    joined = jnp.concatenate([sinusoid(timesteps), pooled.astype(jnp.float32)], axis=1)
    return jax.nn.silu(joined).astype(jnp.bfloat16)


def normalize(values):
    average = jnp.mean(values, axis=1, keepdims=True)
    centred = values - average
    variance = jnp.mean(centred * centred, axis=1, keepdims=True)
    return centred * lax.rsqrt(variance + EPS_NORM)


def modulate(normed, modulation):
    return (normed * (1.0 + modulation[D:]) + modulation[:D]).astype(jnp.bfloat16)


def unembed_part(residual_sum, out_weight):
    return lax.dot_general(
        residual_sum.astype(jnp.bfloat16),
        out_weight,
        (((1,), (1,)), ((), ())),
        preferred_element_type=jnp.float32,
    )


def row_product(hidden, weight_piece):
    return jnp.dot(hidden, weight_piece, preferred_element_type=jnp.float32)


def body(
    gen_noise, renoise, gen_step, renoise_step, text_pooled, embed, mod_weight, proj_weight, unembed
):
    quarter = proj_weight.shape[2]
    col_start = lax.axis_index("mp") * quarter
    blank_text = jnp.zeros_like(text_pooled)
    noisy_vec = condition(renoise_step, text_pooled)
    local_mod = jnp.concatenate(
        [
            jnp.dot(
                condition(gen_step, text_pooled), mod_weight[0], preferred_element_type=jnp.float32
            ),
            jnp.dot(noisy_vec, mod_weight[1], preferred_element_type=jnp.float32),
            jnp.dot(
                condition(renoise_step, blank_text),
                mod_weight[1],
                preferred_element_type=jnp.float32,
            ),
            jnp.dot(noisy_vec, mod_weight[2], preferred_element_type=jnp.float32),
        ],
        axis=0,
    )
    modulation = lax.all_gather(local_mod, "fsdp", axis=1, tiled=True)
    latent = gen_noise[0].reshape(-1, CH)
    latent_bf = latent.astype(jnp.bfloat16)
    token_rows = latent.shape[0]
    embedded = jnp.dot(latent_bf, embed[0], preferred_element_type=jnp.float32)
    gen_hidden = modulate(normalize(embedded), modulation[0])
    gen_part = row_product(gen_hidden, lax.all_gather(proj_weight[0], "fsdp", axis=0, tiled=True))
    gen_cols = lax.dynamic_slice_in_dim(embedded, col_start, quarter, 1)
    clean_part = unembed_part(gen_cols + gen_part, unembed[0]).reshape(-1, 2 * CH)
    clean_lat = lax.psum(clean_part, "mp")
    noise_level = renoise_step[0].astype(jnp.float32) / 1000.0
    noisy_lat = (1.0 - noise_level) * clean_lat + noise_level * renoise[0]
    noisy_bf = noisy_lat.reshape(-1, CH).astype(jnp.bfloat16)
    teacher_in = jnp.dot(noisy_bf, embed[1], preferred_element_type=jnp.float32)
    teacher_norm = normalize(teacher_in)
    cond_hidden = modulate(teacher_norm, modulation[1])
    blank_hidden = modulate(teacher_norm, modulation[2])
    fake_in = jnp.dot(noisy_bf, embed[2], preferred_element_type=jnp.float32)
    fake_hidden = modulate(normalize(fake_in), modulation[3])
    pieces = (
        lax.all_gather(proj_weight[1], "fsdp", axis=0, tiled=True),
        lax.all_gather(proj_weight[2], "fsdp", axis=0, tiled=True),
    )
    cond_part = row_product(cond_hidden, pieces[0])
    blank_part = row_product(blank_hidden, pieces[0])
    fake_part = row_product(fake_hidden, pieces[1])
    teacher_cols = lax.dynamic_slice_in_dim(teacher_in, col_start, quarter, 1)
    fake_cols = lax.dynamic_slice_in_dim(fake_in, col_start, quarter, 1)
    cond_out, blank_out, fake_out = (
        lax.psum(
            unembed_part(teacher_cols + cond_part, unembed[1])
            .reshape(-1, 2 * CH)
            .astype(jnp.bfloat16),
            "mp",
        ).astype(jnp.float32),
        lax.psum(
            unembed_part(teacher_cols + blank_part, unembed[1])
            .reshape(-1, 2 * CH)
            .astype(jnp.bfloat16),
            "mp",
        ).astype(jnp.float32),
        lax.psum(
            unembed_part(fake_cols + fake_part, unembed[2])
            .reshape(-1, 2 * CH)
            .astype(jnp.bfloat16),
            "mp",
        ).astype(jnp.float32),
    )
    real_pred = noisy_lat - noise_level * (blank_out + GUIDANCE * (cond_out - blank_out))
    fake_pred = noisy_lat - noise_level * fake_out
    seq_len = token_rows * lax.axis_size("fsdp")
    gap_total = lax.psum(jnp.sum(jnp.abs(clean_lat - real_pred)), "fsdp")
    gap_scale = gap_total / (seq_len * CH) + EPS_GAP
    score_gap = (fake_pred - real_pred) / gap_scale
    all_tokens = seq_len * lax.axis_size("dp")
    cotangent = (score_gap / math.sqrt(all_tokens)).astype(jnp.bfloat16).reshape(-1, CH)
    upstream = jnp.dot(cotangent, unembed[0], preferred_element_type=jnp.float32).astype(
        jnp.bfloat16
    )
    row_terms = lax.psum_scatter(
        lax.dot_general(
            gen_hidden, upstream, (((0,), (0,)), ((), ())), preferred_element_type=jnp.float32
        ).astype(jnp.bfloat16),
        "fsdp",
        scatter_dimension=0,
        tiled=True,
    )
    gen_grad = lax.psum(row_terms, "dp").astype(jnp.float32)
    return (gen_grad, score_gap[None])


def solution(mesh):
    return jax.shard_map(
        body,
        mesh=mesh,
        in_specs=(
            P("dp", "fsdp", None),
            P("dp", "fsdp", None),
            P("dp"),
            P("dp"),
            P("dp", None),
            P(),
            P(None, None, "fsdp"),
            P(None, "fsdp", "mp"),
            P(None, None, "mp"),
        ),
        out_specs=(P("fsdp", "mp"), P("dp", "fsdp", None)),
        check_vma=False,
    )
```

profile of v0, /device:TPU:2, one launch (start us, length us, event | category | flops | bytes accessed | tf_op | source)
XLA Modules:
  0.0 498.5 jit_solution(18427168380381059458)
XLA Ops:
  7.2 0.0 all-gather.7.cloned.1.call-start
  7.2 2.1 fusion.104
  9.3 0.0 all-gather.7.cloned.1.call-update
  9.3 0.0 all-reduce.5.cloned.1.call-start
  9.4 0.9 convert_element_type.109
  10.3 0.1 convert_element_type.110
  11.7 0.1 fusion.100
  11.8 0.7 convert_reduce_fusion
  12.6 1.3 fusion.49
  13.9 1.3 fusion.53
  15.2 1.3 fusion.51
  16.6 1.3 fusion.55
  17.9 0.1 pad_maximum_fusion
  18.0 23.6 %all_gather.12 = f32[4,6144]{1,0:T(4,128)S(1)} all-gather(f32[4,384]{1,0:T(4,128)S(1)} %pad_maximum_fusion), channel_id=1, replica_groups=mesh['mp'=4,'fsdp'=16,'dp'=4] {'fsdp'}, dimensions={1}, use_global_device_ids=true | all-gather | bytes 104448 | tf_op jit(solution)/shard_map/all_gather | solution.py:73
  41.7 2.1 fusion.105
  43.8 2.6 copy-done
  46.4 0.8 multiply_reduce_fusion.2
  47.2 0.1 slice_add_fusion.1
  47.3 25.2 %all-gather.7.cloned.1.call-done = bf16[1,3072,768]{2,1,0:T(8,128)(2,1)} async-done(((bf16[1,192,768]{2,1,0:T(8,128)(2,1)}), bf16[1,3072,768]{2,1,0:T(8,128)(2,1)}) %all-gather.7.cloned.1.call-update) | async-done | bytes 4718608 | tf_op jit(solution)/shard_map/all_gather | solution.py:79
  72.5 0.0 copy-done.6
  72.5 7.9 %fusion.38 = f32[512,64]{1,0:T(8,128)S(1)} fusion(f32[512,3072]{1,0:T(8,128)} %copy-done, s32[]{:T(128)S(6)} %select_n.2, bf16[1,3072,768]{2,1,0:T(8,128)(2,1)} %all-gather.7.cloned.1.call-done, bf16[3,64,768]{2,1,0:T(8,128)(2,1)S(1)} %copy-done.6, f32[3072]{0:T(1024)S(1)} %bitcast.103, f32[3072]{0:T(1024)S(1)} %bitcast.105, f32[512]{0:T(512)S(1)} %add_rsqrt_fusion.2, ...), kind=kOutput, calls=%fused_computation.36 | convolution fusion | flops 2474901504 | bytes 12840964 | tf_op jit(solution)/shard_map/dot_general | solution.py:39
  80.3 0.8 reshape.200
  81.1 0.0 all-reduce.5.cloned.1.call-update
  81.1 0.0 all-gather.9.cloned.1.call-start
  81.2 0.7 all-gather.9.cloned.1.call-update
  81.8 0.0 all-gather.11.cloned.1.call-start
  81.9 0.5 all-gather.11.cloned.1.call-update
  82.4 0.2 all-reduce.9.cloned.1.call-start
  82.7 38.7 %all-reduce.5.cloned.1.call-done = f32[256,128]{1,0:T(8,128)} async-done(((f32[256,128]{1,0:T(8,128)}), f32[256,128]{1,0:T(8,128)}) %all-reduce.5.cloned.1.call-update) | async-done | bytes 131088 | tf_op jit(solution)/shard_map/psum | solution.py:82
  121.3 0.0 copy-done.4
  121.4 0.9 fusion.85
  122.3 0.1 convert_element_type.120
  122.4 0.0 copy-done.3
  122.4 1.0 fusion.106
  123.4 2.7 copy-done.2
  126.1 0.8 multiply_reduce_fusion.1
  126.9 56.7 %all-gather.9.cloned.1.call-done = bf16[1,3072,768]{2,1,0:T(8,128)(2,1)} async-done(((bf16[1,192,768]{2,1,0:T(8,128)(2,1)}), bf16[1,3072,768]{2,1,0:T(8,128)(2,1)}) %all-gather.9.cloned.1.call-update) | async-done | bytes 4718608 | tf_op jit(solution)/shard_map/all_gather | solution.py:94
  183.6 7.9 %fusion.46 = bf16[512,64]{0,1:T(8,128)(2,1)S(1)} fusion(f32[512,3072]{1,0:T(8,128)} %copy-done.2, s32[]{:T(128)S(6)} %select_n.2, bf16[1,3072,768]{2,1,0:T(8,128)(2,1)} %all-gather.9.cloned.1.call-done, f32[3072]{0:T(1024)S(1)} %bitcast.111, f32[3072]{0:T(1024)S(1)} %bitcast.112, f32[512]{0:T(512)S(1)} %add_rsqrt_fusion.1, ...), kind=kOutput, calls=%fused_computation.39 | convolution fusion | flops 2474934272 | bytes 12775428 | tf_op jit(solution)/shard_map/dot_general | solution.py:39
  191.5 0.1 copy.12
  191.6 0.8 convert_element_type.124
  192.4 1.0 fusion.107
  193.4 2.7 copy-done.1
  196.1 0.8 multiply_reduce_fusion
  196.8 48.7 %all-gather.11.cloned.1.call-done = bf16[1,3072,768]{2,1,0:T(8,128)(2,1)} async-done(((bf16[1,192,768]{2,1,0:T(8,128)(2,1)}), bf16[1,3072,768]{2,1,0:T(8,128)(2,1)}) %all-gather.11.cloned.1.call-update) | async-done | bytes 4718608 | tf_op jit(solution)/shard_map/all_gather | solution.py:93
  245.5 7.9 %fusion.40 = bf16[512,64]{0,1:T(8,128)(2,1)S(1)} fusion(f32[512,3072]{1,0:T(8,128)} %copy-done.1, s32[]{:T(128)S(6)} %select_n.2, bf16[1,3072,768]{2,1,0:T(8,128)(2,1)} %all-gather.11.cloned.1.call-done, f32[3072]{0:T(1024)S(1)} %bitcast.109, f32[3072]{0:T(1024)S(1)} %bitcast.110, f32[512]{0:T(512)S(1)} %add_rsqrt_fusion, ...), kind=kOutput, calls=%fused_computation.37 | convolution fusion | flops 2474934272 | bytes 12775428 | tf_op jit(solution)/shard_map/dot_general | solution.py:39
  253.4 0.1 copy.14
  253.5 0.8 convert_element_type.134
  254.3 7.9 %fusion.43 = bf16[512,64]{0,1:T(8,128)(2,1)S(1)} fusion(f32[512,3072]{1,0:T(8,128)} %copy-done.1, s32[]{:T(128)S(6)} %select_n.2, bf16[1,3072,768]{2,1,0:T(8,128)(2,1)} %all-gather.11.cloned.1.call-done, f32[3072]{0:T(1024)S(1)} %bitcast.108, f32[3072]{0:T(1024)S(1)} %bitcast.107, f32[512]{0:T(512)S(1)} %add_rsqrt_fusion, ...), kind=kOutput, calls=%fused_computation.38 | convolution fusion | flops 2474934272 | bytes 12775428 | tf_op jit(solution)/shard_map/dot_general | solution.py:39
  262.2 0.1 copy.13
  262.4 0.8 convert_element_type.129
  263.1 0.0 all-reduce.9.cloned.1.call-update
  263.1 0.0 reduce-scatter.2.cloned.1.call-start
  263.2 40.5 %all-reduce.9.cloned.1.call-done = (bf16[256,128]{1,0:T(8,128)(2,1)}, bf16[256,128]{1,0:T(8,128)(2,1)}, bf16[256,128]{1,0:T(8,128)(2,1)}) async-done(((bf16[256,128]{1,0:T(8,128)(2,1)}, bf16[256,128]{1,0:T(8,128)(2,1)}, bf16[256,128]{1,0:T(8,128)(2,1)}), (bf16[256,128]{1,0:T(8,128)(2,1)}, bf16[256,128]{1,0:T(8,128)(2,1)}, bf16[256,128]{1,0:T(8,128)(2,1)})) %all-reduce.9.cloned.1.call-update) | async-done | bytes 196624 | tf_op jit(solution)/shard_map/psum | solution.py:114
  303.7 1.5 abs_reduce_fusion
  305.2 37.2 %psum.46 = f32[]{:T(128)} all-reduce(f32[]{:T(128)} %abs_reduce_fusion), channel_id=1, replica_groups=mesh['mp'=4,'fsdp'=16,'dp'=4] {'fsdp'}, use_global_device_ids=true, to_apply=%region_11.12 | all-reduce | flops 1 | bytes 8 | tf_op jit(solution)/shard_map/psum | solution.py:124
  343.1 1.6 multiply_convert_fusion
  344.7 0.1 reshape.201
  344.8 8.2 %convolution_convert_fusion = bf16[3072,768]{1,0:T(8,128)(2,1)} fusion(bf16[512,64]{1,0:T(8,128)(2,1)S(1)} %reshape.201, bf16[3,64,768]{2,1,0:T(8,128)(2,1)S(1)} %copy-done.6, f32[512,3072]{1,0:T(8,128)} %copy-done, f32[3072]{0:T(1024)S(1)} %bitcast.104, f32[3072]{0:T(1024)S(1)} %bitcast.106, f32[512]{0:T(512)S(1)} %add_rsqrt_fusion.2, ...), kind=kOutput, calls=%fused_computation.7 | convolution fusion | flops 2476867584 | bytes 11268096 | tf_op jit(solution)/shard_map/dot_general | solution.py:133
  353.0 0.0 reduce-scatter.2.cloned.1.call-update
  353.0 0.0 all-reduce.7.cloned.1.call-start
  353.1 82.9 %reduce-scatter.2.cloned.1.call-done = bf16[192,768]{1,0:T(8,128)(2,1)} async-done(((bf16[3072,768]{1,0:T(8,128)(2,1)}), bf16[192,768]{1,0:T(8,128)(2,1)}) %reduce-scatter.2.cloned.1.call-update) | async-done | bytes 294928 | tf_op jit(solution)/shard_map/reduce_scatter | solution.py:132
  436.0 0.0 all-reduce.7.cloned.1.call-update
  436.0 53.8 %all-reduce.7.cloned.1.call-done = bf16[192,768]{1,0:T(8,128)(2,1)} async-done(((bf16[192,768]{1,0:T(8,128)(2,1)}), bf16[192,768]{1,0:T(8,128)(2,1)}) %all-reduce.7.cloned.1.call-update) | async-done | bytes 294928 | tf_op jit(solution)/shard_map/psum | solution.py:140
  489.8 1.8 convert_element_type.139
  (20 shorter events, 0.1 us)
Async XLA Ops:
  7.2 65.3 %all-gather.7.cloned.1.call-start = ((), (), s32[]{:S(2)}) async-start(), calls=%async_computation.4 | async-start | bytes 5013504 | tf_op jit(solution)/shard_map/all_gather | solution.py:79
  9.3 112.0 %all-reduce.5.cloned.1.call-start = ((), (), s32[]{:S(2)}) async-start(), calls=%async_computation.1 | async-start | bytes 262144 | tf_op jit(solution)/shard_map/psum | solution.py:82
  41.7 30.8 %copy-start.6 = (bf16[3,64,768]{2,1,0:T(8,128)(2,1)S(1)}, bf16[3,64,768]{2,1,0:T(8,128)(2,1)}, u32[]{:S(2)}) copy-start(bf16[3,64,768]{2,1,0:T(8,128)(2,1)} %param.17) | copy-start | bytes 884740
  43.7 2.7 copy-start
  72.5 48.9 %copy-start.4 = (f32[1,256,128]{2,1,0:T(8,128)S(1)}, f32[1,256,128]{2,1,0:T(8,128)}, u32[]{:S(2)}) copy-start(f32[1,256,128]{2,1,0:T(8,128)} %param.10) | copy-start | bytes 393220
  72.5 49.9 %copy-start.3 = (bf16[3,64,3072]{2,1,0:T(8,128)(2,1)S(1)}, bf16[3,64,3072]{2,1,0:T(8,128)(2,1)}, u32[]{:S(2)}) copy-start(bf16[3,64,3072]{2,1,0:T(8,128)(2,1)} %param.14) | copy-start | bytes 3538948
  81.1 102.4 %all-gather.9.cloned.1.call-start = ((), (), s32[]{:S(2)}) async-start(), calls=%async_computation.5 | async-start | bytes 5013504 | tf_op jit(solution)/shard_map/all_gather | solution.py:94
  81.8 163.7 %all-gather.11.cloned.1.call-start = ((), (), s32[]{:S(2)}) async-start(), calls=%async_computation.6 | async-start | bytes 5013504 | tf_op jit(solution)/shard_map/all_gather | solution.py:93
  82.4 221.2 %all-reduce.9.cloned.1.call-start = ((), (), s32[]{:S(2)}) async-start(), calls=%async_computation.7 | async-start | bytes 393216 | tf_op jit(solution)/shard_map/psum | solution.py:114
  123.4 2.7 copy-start.2
  193.4 2.7 copy-start.1
  254.3 49.4 %copy-start.5 = (f32[256,128]{1,0:T(8,128)S(1)}, f32[256,128]{1,0:T(8,128)}, u32[]{:S(2)}) copy-start(f32[256,128]{1,0:T(8,128)} %all-reduce.5.cloned.1.call-done) | copy-start | bytes 393220
  263.1 172.8 %reduce-scatter.2.cloned.1.call-start = ((), (), s32[]{:S(2)}) async-start(), calls=%async_computation.2 | async-start | bytes 5013504 | tf_op jit(solution)/shard_map/reduce_scatter | solution.py:132
  353.0 136.8 %all-reduce.7.cloned.1.call-start = ((), (), s32[]{:S(2)}) async-start(), calls=%async_computation.3 | async-start | bytes 589824 | tf_op jit(solution)/shard_map/psum | solution.py:140
Sparse Core Ops, SparseCore 0:
  10.4 61.9 all-gather.6
  81.2 40.0 all-reduce.4
  124.1 59.4 all-gather.8
  186.7 58.7 all-gather.10
  263.3 40.3 all-reduce.8
  353.2 82.7 reduce-scatter.1
  438.6 51.1 all-reduce.6
where the time goes:
time: 499 us; the launch traced here: 498 us
  waiting for transfers between devices  348 us (70%)
  blocking collectives  60.9 us (12%)
  matrix products  49.3 us (10%)
  between operations  16.3 us (3%)
  local copies, waits for them, and re-layouts  13.7 us (3%)
  other arithmetic  10.1 us (2%)
    reduce_scatter x1, waiting for transfers between devices, body(): lax.psum_scatter(lax.dot_general(gen_hidden, upstream, (((0,), (0,)), (()...  82.9 us
    all_gather x1, waiting for transfers between devices, body(): lax.all_gather(proj_weight[2], 'fsdp', axis=0, tiled=True)  56.7 us
    psum x1, waiting for transfers between devices, body(): gen_grad = lax.psum(row_terms, 'dp').astype(jnp.float32)  53.8 us
    all_gather x1, waiting for transfers between devices, body(): lax.all_gather(proj_weight[1], 'fsdp', axis=0, tiled=True)  48.7 us
    psum x1, waiting for transfers between devices, body(): lax.psum(unembed_part(fake_cols + fake_part, unembed[2]).reshape(-1, 2 *...  40.5 us
    psum x1, waiting for transfers between devices, body(): clean_lat = lax.psum(clean_part, 'mp')  38.7 us
    psum x1, blocking collectives, body(): gap_total = lax.psum(jnp.sum(jnp.abs(clean_lat - real_pred)), 'fsdp')  37.2 us
    dot_general x4, matrix products, unembed_part(): lax.dot_general(residual_sum.astype(jnp.bfloat16), out_weight, (((1,), (1...  31.6 us
  transfers between devices with their start and end apart: 7, of which 7 were waited for; matrix products, arithmetic and copies ran while one was open for 5% of the time, Pallas kernels for 0%

commit v1 on v0

--- a/solution.py
+++ b/solution.py
@@ -70,7 +70,12 @@
         ],
         axis=0,
     )
-    modulation = lax.all_gather(local_mod, "fsdp", axis=1, tiled=True)
+    ring = [local_mod]
+    for hop in range(15):
+        ring.append(lax.ppermute(ring[-1], "fsdp", [(dev, (dev + 1) % 16) for dev in range(16)]))
+    modulation = jnp.roll(
+        jnp.concatenate(ring[::-1], axis=1), (lax.axis_index("fsdp") + 1) * ring[0].shape[1], axis=1
+    )
     latent = gen_noise[0].reshape(-1, CH)
     latent_bf = latent.astype(jnp.bfloat16)
     token_rows = latent.shape[0]

time: 499 us -> 547 us (1.096)
  waiting for transfers between devices: 348 us -> 419 us
  blocking collectives: 60.9 us -> 37.3 us
    ppermute x0 -> x15, waiting for transfers between devices: none -> 94.9 us  [body(): lax.ppermute(ring[-1], 'fsdp', [(dev, (dev + 1) % 16) for dev in range(16)])]
    all_gather x1, waiting for transfers between devices: 25.2 us -> 0.02 us  [body(): lax.all_gather(proj_weight[0], 'fsdp', axis=0, tiled=True)]
    all_gather x1 -> x0, blocking collectives: 23.6 us -> none  [body(): modulation = lax.all_gather(local_mod, 'fsdp', axis=1, tiled=True)]
  transfers between devices with their start and end apart: 7 -> 22, of which waited for: 7 -> 21; matrix products, arithmetic and copies ran while one was open for 5% -> 4% of each run, Pallas kernels for 0% -> 0%
where the time goes in v1:
time: 547 us; the launch traced here: 546 us
  waiting for transfers between devices  419 us (77%)
  matrix products  49.2 us (9%)
  blocking collectives  37.3 us (7%)
  between operations  16.4 us (3%)
  local copies, waits for them, and re-layouts  11.3 us (2%)
  other arithmetic  10.3 us (2%)
    ppermute x15, waiting for transfers between devices, body(): lax.ppermute(ring[-1], 'fsdp', [(dev, (dev + 1) % 16) for dev in range(16)])  94.9 us
    reduce_scatter x1, waiting for transfers between devices, body(): lax.psum_scatter(lax.dot_general(gen_hidden, upstream, (((0,), (0,)), (()...  82.7 us
    all_gather x1, waiting for transfers between devices, body(): lax.all_gather(proj_weight[2], 'fsdp', axis=0, tiled=True)  56.7 us
    psum x1, waiting for transfers between devices, body(): gen_grad = lax.psum(row_terms, 'dp').astype(jnp.float32)  53.8 us
    all_gather x1, waiting for transfers between devices, body(): lax.all_gather(proj_weight[1], 'fsdp', axis=0, tiled=True)  48.7 us
    psum x1, waiting for transfers between devices, body(): lax.psum(unembed_part(fake_cols + fake_part, unembed[2]).reshape(-1, 2 *...  40.5 us
    psum x1, waiting for transfers between devices, body(): clean_lat = lax.psum(clean_part, 'mp')  39.9 us
    psum x1, blocking collectives, body(): gap_total = lax.psum(jnp.sum(jnp.abs(clean_lat - real_pred)), 'fsdp')  37.3 us
  transfers between devices with their start and end apart: 22, of which 21 were waited for; matrix products, arithmetic and copies ran while one was open for 4% of the time, Pallas kernels for 0%

profile of v1, /device:TPU:2, one launch (start us, length us, event | category | flops | bytes accessed | tf_op | source)
XLA Modules:
  0.0 546.5 jit_solution(10075132419414955396)
XLA Ops:
  7.2 2.1 fusion.104
  10.7 0.1 fusion.100
  10.8 0.7 convert_reduce_fusion
  11.6 1.3 fusion.49
  12.9 1.3 fusion.53
  14.2 1.3 fusion.51
  15.6 1.3 fusion.55
  16.9 0.1 pad_maximum_fusion
  17.0 1.6 collective-permute-start
  18.6 2.4 collective-permute-done
  21.0 1.2 collective-permute-start.1
  22.2 5.7 %collective-permute-done.1 = f32[4,384]{1,0:T(4,128)S(1)} collective-permute-done((f32[4,384]{1,0:T(4,128)S(1)}, f32[4,384]{1,0:T(4,128)S(1)}, u32[]{:S(2)}, u32[]{:S(2)}) %collective-permute-start.1) | collective-permute-done | bytes 6176 | tf_op jit(solution)/shard_map/ppermute | solution.py:75
  27.9 6.9 %collective-permute-done.2 = f32[4,384]{1,0:T(4,128)S(1)} collective-permute-done((f32[4,384]{1,0:T(4,128)S(1)}, f32[4,384]{1,0:T(4,128)S(1)}, u32[]{:S(2)}, u32[]{:S(2)}) %collective-permute-start.2) | collective-permute-done | bytes 6176 | tf_op jit(solution)/shard_map/ppermute | solution.py:75
  34.9 7.0 %collective-permute-done.3 = f32[4,384]{1,0:T(4,128)S(1)} collective-permute-done((f32[4,384]{1,0:T(4,128)S(1)}, f32[4,384]{1,0:T(4,128)S(1)}, u32[]{:S(2)}, u32[]{:S(2)}) %collective-permute-start.3) | collective-permute-done | bytes 6176 | tf_op jit(solution)/shard_map/ppermute | solution.py:75
  41.8 6.9 %collective-permute-done.4 = f32[4,384]{1,0:T(4,128)S(1)} collective-permute-done((f32[4,384]{1,0:T(4,128)S(1)}, f32[4,384]{1,0:T(4,128)S(1)}, u32[]{:S(2)}, u32[]{:S(2)}) %collective-permute-start.4) | collective-permute-done | bytes 6176 | tf_op jit(solution)/shard_map/ppermute | solution.py:75
  48.8 7.2 %collective-permute-done.5 = f32[4,384]{1,0:T(4,128)S(1)} collective-permute-done((f32[4,384]{1,0:T(4,128)S(1)}, f32[4,384]{1,0:T(4,128)S(1)}, u32[]{:S(2)}, u32[]{:S(2)}) %collective-permute-start.5) | collective-permute-done | bytes 6176 | tf_op jit(solution)/shard_map/ppermute | solution.py:75
  55.9 7.0 %collective-permute-done.6 = f32[4,384]{1,0:T(4,128)S(1)} collective-permute-done((f32[4,384]{1,0:T(4,128)S(1)}, f32[4,384]{1,0:T(4,128)S(1)}, u32[]{:S(2)}, u32[]{:S(2)}) %collective-permute-start.6) | collective-permute-done | bytes 6176 | tf_op jit(solution)/shard_map/ppermute | solution.py:75
  62.9 7.0 %collective-permute-done.7 = f32[4,384]{1,0:T(4,128)S(1)} collective-permute-done((f32[4,384]{1,0:T(4,128)S(1)}, f32[4,384]{1,0:T(4,128)S(1)}, u32[]{:S(2)}, u32[]{:S(2)}) %collective-permute-start.7) | collective-permute-done | bytes 6176 | tf_op jit(solution)/shard_map/ppermute | solution.py:75
  69.9 7.0 %collective-permute-done.8 = f32[4,384]{1,0:T(4,128)S(1)} collective-permute-done((f32[4,384]{1,0:T(4,128)S(1)}, f32[4,384]{1,0:T(4,128)S(1)}, u32[]{:S(2)}, u32[]{:S(2)}) %collective-permute-start.8) | collective-permute-done | bytes 6176 | tf_op jit(solution)/shard_map/ppermute | solution.py:75
  76.9 6.9 %collective-permute-done.9 = f32[4,384]{1,0:T(4,128)S(1)} collective-permute-done((f32[4,384]{1,0:T(4,128)S(1)}, f32[4,384]{1,0:T(4,128)S(1)}, u32[]{:S(2)}, u32[]{:S(2)}) %collective-permute-start.9) | collective-permute-done | bytes 6176 | tf_op jit(solution)/shard_map/ppermute | solution.py:75
  83.8 0.9 convert_element_type.109
  84.7 0.1 convert_element_type.110
  84.9 5.9 %collective-permute-done.10 = f32[4,384]{1,0:T(4,128)S(1)} collective-permute-done((f32[4,384]{1,0:T(4,128)S(1)}, f32[4,384]{1,0:T(4,128)S(1)}, u32[]{:S(2)}, u32[]{:S(2)}) %collective-permute-start.10) | collective-permute-done | bytes 6176 | tf_op jit(solution)/shard_map/ppermute | solution.py:75
  90.8 2.0 fusion.105
  92.8 4.9 collective-permute-done.11
  97.7 6.9 %collective-permute-done.12 = f32[4,384]{1,0:T(4,128)S(1)} collective-permute-done((f32[4,384]{1,0:T(4,128)S(1)}, f32[4,384]{1,0:T(4,128)S(1)}, u32[]{:S(2)}, u32[]{:S(2)}) %collective-permute-start.12) | collective-permute-done | bytes 6176 | tf_op jit(solution)/shard_map/ppermute | solution.py:75
  104.7 0.8 multiply_reduce_fusion.2
  105.4 6.2 %collective-permute-done.13 = f32[4,384]{1,0:T(4,128)S(1)} collective-permute-done((f32[4,384]{1,0:T(4,128)S(1)}, f32[4,384]{1,0:T(4,128)S(1)}, u32[]{:S(2)}, u32[]{:S(2)}) %collective-permute-start.13) | collective-permute-done | bytes 6176 | tf_op jit(solution)/shard_map/ppermute | solution.py:75
  111.6 6.9 %collective-permute-done.14 = f32[4,384]{1,0:T(4,128)S(1)} collective-permute-done((f32[4,384]{1,0:T(4,128)S(1)}, f32[4,384]{1,0:T(4,128)S(1)}, u32[]{:S(2)}, u32[]{:S(2)}) %collective-permute-start.14) | collective-permute-done | bytes 6176 | tf_op jit(solution)/shard_map/ppermute | solution.py:75
  119.0 0.3 dynamic-slice_add_fusion.1
  119.3 7.9 %fusion.38 = f32[512,64]{1,0:T(8,128)S(1)} fusion(f32[512,3072]{1,0:T(8,128)} %copy-done, s32[]{:T(128)S(6)} %select_n.20, bf16[1,3072,768]{2,1,0:T(8,128)(2,1)} %all-gather.7.cloned.1.call-done, bf16[3,64,768]{2,1,0:T(8,128)(2,1)S(1)} %copy-done.6, f32[3072]{0:T(1024)S(1)} %bitcast.103, f32[3072]{0:T(1024)S(1)} %bitcast.105, f32[512]{0:T(512)S(1)} %add_rsqrt_fusion.2, ...), kind=kOutput, calls=%fused_computation.36 | convolution fusion | flops 2474901504 | bytes 12840964 | tf_op jit(solution)/shard_map/dot_general | solution.py:39
  127.2 0.8 reshape.200
  128.0 0.7 all-gather.9.cloned.1.call-update
  128.8 0.5 all-gather.11.cloned.1.call-update
  129.3 0.3 all-reduce.9.cloned.1.call-start
  129.6 39.9 %all-reduce.5.cloned.1.call-done = f32[256,128]{1,0:T(8,128)} async-done(((f32[256,128]{1,0:T(8,128)}), f32[256,128]{1,0:T(8,128)}) %all-reduce.5.cloned.1.call-update) | async-done | bytes 131088 | tf_op jit(solution)/shard_map/psum | solution.py:87
  169.5 0.9 fusion.85
  170.4 0.1 convert_element_type.120
  170.5 1.0 fusion.106
  171.6 2.6 copy-done.2
  174.2 0.8 multiply_reduce_fusion.1
  175.0 56.7 %all-gather.9.cloned.1.call-done = bf16[1,3072,768]{2,1,0:T(8,128)(2,1)} async-done(((bf16[1,192,768]{2,1,0:T(8,128)(2,1)}), bf16[1,3072,768]{2,1,0:T(8,128)(2,1)}) %all-gather.9.cloned.1.call-update) | async-done | bytes 4718608 | tf_op jit(solution)/shard_map/all_gather | solution.py:99
  231.7 7.9 %fusion.46 = bf16[512,64]{0,1:T(8,128)(2,1)S(1)} fusion(f32[512,3072]{1,0:T(8,128)} %copy-done.2, s32[]{:T(128)S(6)} %select_n.20, bf16[1,3072,768]{2,1,0:T(8,128)(2,1)} %all-gather.9.cloned.1.call-done, f32[3072]{0:T(1024)S(1)} %bitcast.111, f32[3072]{0:T(1024)S(1)} %bitcast.112, f32[512]{0:T(512)S(1)} %add_rsqrt_fusion.1, ...), kind=kOutput, calls=%fused_computation.39 | convolution fusion | flops 2474934272 | bytes 12775428 | tf_op jit(solution)/shard_map/dot_general | solution.py:39
  239.6 0.1 copy.12
  239.7 0.8 convert_element_type.124
  240.5 1.0 fusion.107
  241.6 2.6 copy-done.1
  244.2 0.8 multiply_reduce_fusion
  245.0 48.7 %all-gather.11.cloned.1.call-done = bf16[1,3072,768]{2,1,0:T(8,128)(2,1)} async-done(((bf16[1,192,768]{2,1,0:T(8,128)(2,1)}), bf16[1,3072,768]{2,1,0:T(8,128)(2,1)}) %all-gather.11.cloned.1.call-update) | async-done | bytes 4718608 | tf_op jit(solution)/shard_map/all_gather | solution.py:98
  293.7 7.9 %fusion.40 = bf16[512,64]{0,1:T(8,128)(2,1)S(1)} fusion(f32[512,3072]{1,0:T(8,128)} %copy-done.1, s32[]{:T(128)S(6)} %select_n.20, bf16[1,3072,768]{2,1,0:T(8,128)(2,1)} %all-gather.11.cloned.1.call-done, f32[3072]{0:T(1024)S(1)} %bitcast.110, f32[3072]{0:T(1024)S(1)} %bitcast.109, f32[512]{0:T(512)S(1)} %add_rsqrt_fusion, ...), kind=kOutput, calls=%fused_computation.37 | convolution fusion | flops 2474934272 | bytes 12775428 | tf_op jit(solution)/shard_map/dot_general | solution.py:39
  301.6 0.1 copy.14
  301.7 0.8 convert_element_type.134
  302.4 7.9 %fusion.43 = bf16[512,64]{0,1:T(8,128)(2,1)S(1)} fusion(f32[512,3072]{1,0:T(8,128)} %copy-done.1, s32[]{:T(128)S(6)} %select_n.20, bf16[1,3072,768]{2,1,0:T(8,128)(2,1)} %all-gather.11.cloned.1.call-done, f32[3072]{0:T(1024)S(1)} %bitcast.108, f32[3072]{0:T(1024)S(1)} %bitcast.107, f32[512]{0:T(512)S(1)} %add_rsqrt_fusion, ...), kind=kOutput, calls=%fused_computation.38 | convolution fusion | flops 2474934272 | bytes 12775428 | tf_op jit(solution)/shard_map/dot_general | solution.py:39
  310.4 0.1 copy.13
  310.5 0.7 convert_element_type.129
  311.3 40.5 %all-reduce.9.cloned.1.call-done = (bf16[256,128]{1,0:T(8,128)(2,1)}, bf16[256,128]{1,0:T(8,128)(2,1)}, bf16[256,128]{1,0:T(8,128)(2,1)}) async-done(((bf16[256,128]{1,0:T(8,128)(2,1)}, bf16[256,128]{1,0:T(8,128)(2,1)}, bf16[256,128]{1,0:T(8,128)(2,1)}), (bf16[256,128]{1,0:T(8,128)(2,1)}, bf16[256,128]{1,0:T(8,128)(2,1)}, bf16[256,128]{1,0:T(8,128)(2,1)})) %all-reduce.9.cloned.1.call-update) | async-done | bytes 196624 | tf_op jit(solution)/shard_map/psum | solution.py:119
  351.8 1.5 abs_reduce_fusion
  353.3 37.3 %psum.46 = f32[]{:T(128)} all-reduce(f32[]{:T(128)} %abs_reduce_fusion), channel_id=1, replica_groups=mesh['mp'=4,'fsdp'=16,'dp'=4] {'fsdp'}, use_global_device_ids=true, to_apply=%region_11.12 | all-reduce | flops 1 | bytes 8 | tf_op jit(solution)/shard_map/psum | solution.py:129
  391.3 1.6 multiply_convert_fusion
  392.9 0.1 reshape.201
  393.0 8.2 %convolution_convert_fusion = bf16[3072,768]{1,0:T(8,128)(2,1)} fusion(bf16[512,64]{1,0:T(8,128)(2,1)S(1)} %reshape.201, bf16[3,64,768]{2,1,0:T(8,128)(2,1)S(1)} %copy-done.6, f32[512,3072]{1,0:T(8,128)} %copy-done, f32[3072]{0:T(1024)S(1)} %bitcast.104, f32[3072]{0:T(1024)S(1)} %bitcast.106, f32[512]{0:T(512)S(1)} %add_rsqrt_fusion.2, ...), kind=kOutput, calls=%fused_computation.7 | convolution fusion | flops 2476867584 | bytes 11268096 | tf_op jit(solution)/shard_map/dot_general | solution.py:138
  401.3 82.7 %reduce-scatter.2.cloned.1.call-done = bf16[192,768]{1,0:T(8,128)(2,1)} async-done(((bf16[3072,768]{1,0:T(8,128)(2,1)}), bf16[192,768]{1,0:T(8,128)(2,1)}) %reduce-scatter.2.cloned.1.call-update) | async-done | bytes 294928 | tf_op jit(solution)/shard_map/reduce_scatter | solution.py:137
  484.0 53.8 %all-reduce.7.cloned.1.call-done = bf16[192,768]{1,0:T(8,128)(2,1)} async-done(((bf16[192,768]{1,0:T(8,128)(2,1)}), bf16[192,768]{1,0:T(8,128)(2,1)}) %all-reduce.7.cloned.1.call-update) | async-done | bytes 294928 | tf_op jit(solution)/shard_map/psum | solution.py:145
  537.8 1.8 convert_element_type.139
  (81 shorter events, 0.8 us)
Async XLA Ops:
  7.2 112.1 %all-gather.7.cloned.1.call-start = ((), (), s32[]{:S(2)}) async-start(), calls=%async_computation.4 | async-start | bytes 5013504 | tf_op jit(solution)/shard_map/all_gather | solution.py:84
  9.3 160.2 %all-reduce.5.cloned.1.call-start = ((), (), s32[]{:S(2)}) async-start(), calls=%async_computation.1 | async-start | bytes 262144 | tf_op jit(solution)/shard_map/psum | solution.py:87
  17.0 4.0 collective-permute-start
  21.0 6.9 %collective-permute-start.1 = (f32[4,384]{1,0:T(4,128)S(1)}, f32[4,384]{1,0:T(4,128)S(1)}, u32[]{:S(2)}, u32[]{:S(2)}) collective-permute-start(f32[4,384]{1,0:T(4,128)S(1)} %collective-permute-done), channel_id=1, source_target_pairs={{0,4},{4,8},{8,12},{12,16},{16,20},{20,24},{24,28},{28,32},{32,36}... | collective-permute-start | bytes 18440 | tf_op jit(solution)/shard_map/ppermute | solution.py:75
  27.9 6.9 %collective-permute-start.2 = (f32[4,384]{1,0:T(4,128)S(1)}, f32[4,384]{1,0:T(4,128)S(1)}, u32[]{:S(2)}, u32[]{:S(2)}) collective-permute-start(f32[4,384]{1,0:T(4,128)S(1)} %collective-permute-done.1), channel_id=1, source_target_pairs={{0,4},{4,8},{8,12},{12,16},{16,20},{20,24},{24,28},{28,32},{32,36}... | collective-permute-start | bytes 18440 | tf_op jit(solution)/shard_map/ppermute | solution.py:75
  34.8 7.0 %collective-permute-start.3 = (f32[4,384]{1,0:T(4,128)S(1)}, f32[4,384]{1,0:T(4,128)S(1)}, u32[]{:S(2)}, u32[]{:S(2)}) collective-permute-start(f32[4,384]{1,0:T(4,128)S(1)} %collective-permute-done.2), channel_id=1, source_target_pairs={{0,4},{4,8},{8,12},{12,16},{16,20},{20,24},{24,28},{28,32},{32,36}... | collective-permute-start | bytes 18440 | tf_op jit(solution)/shard_map/ppermute | solution.py:75
  41.8 7.0 %collective-permute-start.4 = (f32[4,384]{1,0:T(4,128)S(1)}, f32[4,384]{1,0:T(4,128)S(1)}, u32[]{:S(2)}, u32[]{:S(2)}) collective-permute-start(f32[4,384]{1,0:T(4,128)S(1)} %collective-permute-done.3), channel_id=1, source_target_pairs={{0,4},{4,8},{8,12},{12,16},{16,20},{20,24},{24,28},{28,32},{32,36}... | collective-permute-start | bytes 18440 | tf_op jit(solution)/shard_map/ppermute | solution.py:75
  48.8 7.2 %collective-permute-start.5 = (f32[4,384]{1,0:T(4,128)S(1)}, f32[4,384]{1,0:T(4,128)S(1)}, u32[]{:S(2)}, u32[]{:S(2)}) collective-permute-start(f32[4,384]{1,0:T(4,128)S(1)} %collective-permute-done.4), channel_id=1, source_target_pairs={{0,4},{4,8},{8,12},{12,16},{16,20},{20,24},{24,28},{28,32},{32,36}... | collective-permute-start | bytes 18440 | tf_op jit(solution)/shard_map/ppermute | solution.py:75
  55.9 7.0 %collective-permute-start.6 = (f32[4,384]{1,0:T(4,128)S(1)}, f32[4,384]{1,0:T(4,128)S(1)}, u32[]{:S(2)}, u32[]{:S(2)}) collective-permute-start(f32[4,384]{1,0:T(4,128)S(1)} %collective-permute-done.5), channel_id=1, source_target_pairs={{0,4},{4,8},{8,12},{12,16},{16,20},{20,24},{24,28},{28,32},{32,36}... | collective-permute-start | bytes 18440 | tf_op jit(solution)/shard_map/ppermute | solution.py:75
  62.9 7.0 %collective-permute-start.7 = (f32[4,384]{1,0:T(4,128)S(1)}, f32[4,384]{1,0:T(4,128)S(1)}, u32[]{:S(2)}, u32[]{:S(2)}) collective-permute-start(f32[4,384]{1,0:T(4,128)S(1)} %collective-permute-done.6), channel_id=1, source_target_pairs={{0,4},{4,8},{8,12},{12,16},{16,20},{20,24},{24,28},{28,32},{32,36}... | collective-permute-start | bytes 18440 | tf_op jit(solution)/shard_map/ppermute | solution.py:75
  69.9 7.0 %collective-permute-start.8 = (f32[4,384]{1,0:T(4,128)S(1)}, f32[4,384]{1,0:T(4,128)S(1)}, u32[]{:S(2)}, u32[]{:S(2)}) collective-permute-start(f32[4,384]{1,0:T(4,128)S(1)} %collective-permute-done.7), channel_id=1, source_target_pairs={{0,4},{4,8},{8,12},{12,16},{16,20},{20,24},{24,28},{28,32},{32,36}... | collective-permute-start | bytes 18440 | tf_op jit(solution)/shard_map/ppermute | solution.py:75
  76.9 6.9 %collective-permute-start.9 = (f32[4,384]{1,0:T(4,128)S(1)}, f32[4,384]{1,0:T(4,128)S(1)}, u32[]{:S(2)}, u32[]{:S(2)}) collective-permute-start(f32[4,384]{1,0:T(4,128)S(1)} %collective-permute-done.8), channel_id=1, source_target_pairs={{0,4},{4,8},{8,12},{12,16},{16,20},{20,24},{24,28},{28,32},{32,36}... | collective-permute-start | bytes 18440 | tf_op jit(solution)/shard_map/ppermute | solution.py:75
  83.8 6.9 %collective-permute-start.10 = (f32[4,384]{1,0:T(4,128)S(1)}, f32[4,384]{1,0:T(4,128)S(1)}, u32[]{:S(2)}, u32[]{:S(2)}) collective-permute-start(f32[4,384]{1,0:T(4,128)S(1)} %collective-permute-done.9), channel_id=1, source_target_pairs={{0,4},{4,8},{8,12},{12,16},{16,20},{20,24},{24,28},{28,32},{32,36}... | collective-permute-start | bytes 18440 | tf_op jit(solution)/shard_map/ppermute | solution.py:75
  84.9 34.4 %copy-start.6 = (bf16[3,64,768]{2,1,0:T(8,128)(2,1)S(1)}, bf16[3,64,768]{2,1,0:T(8,128)(2,1)}, u32[]{:S(2)}) copy-start(bf16[3,64,768]{2,1,0:T(8,128)(2,1)} %param.17) | copy-start | bytes 884740
  90.8 6.9 %collective-permute-start.11 = (f32[4,384]{1,0:T(4,128)S(1)}, f32[4,384]{1,0:T(4,128)S(1)}, u32[]{:S(2)}, u32[]{:S(2)}) collective-permute-start(f32[4,384]{1,0:T(4,128)S(1)} %collective-permute-done.10), channel_id=1, source_target_pairs={{0,4},{4,8},{8,12},{12,16},{16,20},{20,24},{24,28},{28,32},{32,36}... | collective-permute-start | bytes 18440 | tf_op jit(solution)/shard_map/ppermute | solution.py:75
  92.8 11.9 %copy-start = (f32[512,3072]{1,0:T(8,128)}, f32[512,3072]{1,0:T(8,128)S(1)}, u32[]{:S(2)}) copy-start(f32[512,3072]{1,0:T(8,128)S(1)} %get-tuple-element.22) | copy-start | bytes 18874372
  97.7 6.9 %collective-permute-start.12 = (f32[4,384]{1,0:T(4,128)S(1)}, f32[4,384]{1,0:T(4,128)S(1)}, u32[]{:S(2)}, u32[]{:S(2)}) collective-permute-start(f32[4,384]{1,0:T(4,128)S(1)} %collective-permute-done.11), channel_id=1, source_target_pairs={{0,4},{4,8},{8,12},{12,16},{16,20},{20,24},{24,28},{28,32},{32,36}... | collective-permute-start | bytes 18440 | tf_op jit(solution)/shard_map/ppermute | solution.py:75
  104.7 7.0 %collective-permute-start.13 = (f32[4,384]{1,0:T(4,128)S(1)}, f32[4,384]{1,0:T(4,128)S(1)}, u32[]{:S(2)}, u32[]{:S(2)}) collective-permute-start(f32[4,384]{1,0:T(4,128)S(1)} %collective-permute-done.12), channel_id=1, source_target_pairs={{0,4},{4,8},{8,12},{12,16},{16,20},{20,24},{24,28},{28,32},{32,36}... | collective-permute-start | bytes 18440 | tf_op jit(solution)/shard_map/ppermute | solution.py:75
  111.6 6.9 %collective-permute-start.14 = (f32[4,384]{1,0:T(4,128)S(1)}, f32[4,384]{1,0:T(4,128)S(1)}, u32[]{:S(2)}, u32[]{:S(2)}) collective-permute-start(f32[4,384]{1,0:T(4,128)S(1)} %collective-permute-done.13), channel_id=1, source_target_pairs={{0,4},{4,8},{8,12},{12,16},{16,20},{20,24},{24,28},{28,32},{32,36}... | collective-permute-start | bytes 18440 | tf_op jit(solution)/shard_map/ppermute | solution.py:75
  119.3 50.2 %copy-start.4 = (f32[1,256,128]{2,1,0:T(8,128)S(1)}, f32[1,256,128]{2,1,0:T(8,128)}, u32[]{:S(2)}) copy-start(f32[1,256,128]{2,1,0:T(8,128)} %param.10) | copy-start | bytes 393220
  119.3 51.2 %copy-start.3 = (bf16[3,64,3072]{2,1,0:T(8,128)(2,1)S(1)}, bf16[3,64,3072]{2,1,0:T(8,128)(2,1)}, u32[]{:S(2)}) copy-start(bf16[3,64,3072]{2,1,0:T(8,128)(2,1)} %param.14) | copy-start | bytes 3538948
  128.0 103.7 %all-gather.9.cloned.1.call-start = ((), (), s32[]{:S(2)}) async-start(), calls=%async_computation.5 | async-start | bytes 5013504 | tf_op jit(solution)/shard_map/all_gather | solution.py:99
  128.7 165.0 %all-gather.11.cloned.1.call-start = ((), (), s32[]{:S(2)}) async-start(), calls=%async_computation.6 | async-start | bytes 5013504 | tf_op jit(solution)/shard_map/all_gather | solution.py:98
  129.3 222.5 %all-reduce.9.cloned.1.call-start = ((), (), s32[]{:S(2)}) async-start(), calls=%async_computation.7 | async-start | bytes 393216 | tf_op jit(solution)/shard_map/psum | solution.py:119
  171.6 2.6 copy-start.2
  241.5 2.6 copy-start.1
  302.4 49.4 %copy-start.5 = (f32[256,128]{1,0:T(8,128)S(1)}, f32[256,128]{1,0:T(8,128)}, u32[]{:S(2)}) copy-start(f32[256,128]{1,0:T(8,128)} %all-reduce.5.cloned.1.call-done) | copy-start | bytes 393220
  311.3 172.7 %reduce-scatter.2.cloned.1.call-start = ((), (), s32[]{:S(2)}) async-start(), calls=%async_computation.2 | async-start | bytes 5013504 | tf_op jit(solution)/shard_map/reduce_scatter | solution.py:137
  401.2 136.6 %all-reduce.7.cloned.1.call-start = ((), (), s32[]{:S(2)}) async-start(), calls=%async_computation.3 | async-start | bytes 589824 | tf_op jit(solution)/shard_map/psum | solution.py:145
Sparse Core Ops, SparseCore 0:
  10.4 61.9 all-gather.6
  128.1 41.3 all-reduce.4
  172.2 59.4 all-gather.8
  234.9 58.7 all-gather.10
  311.4 40.3 all-reduce.8
  401.3 82.5 reduce-scatter.1
  486.6 51.1 all-reduce.6
